TPU v7x, 256 devices: a whole 4x4x8 slice. The times are simulated.
256 devices in a mesh: strat: 32 (over z, y_hi, core), grp: 8 (over x, y_lo).
Axes of the slice: x: 4, y: 4 (y_hi: 2, y_lo: 2; y = y_hi * 2 + y_lo), z: 8, core: 2. Of those that a mesh axis runs over, the one named last changes fastest.
Arguments:
- user_factors: float32 [262144, 256], P(('strat', 'grp')), may hold values from -1.5 to 1.5
- item_factors: float32 [131072, 256], P('strat'), may hold values from -1.5 to 1.5
- tile_coords: int32 [32, 8, 3, 2, 16], P('strat', 'grp'), may hold values from 0 to 31, as said below
- tile_counts: int32 [32, 8, 3], P('strat', 'grp'), may hold values from 5 to 16, as said below
- tile_values: bfloat16 [32, 8, 3, 16, 128, 128], P('strat', 'grp'), may hold values from 0 to 10
Outputs:
- users_out: float32 [262144, 256], P(('strat', 'grp'))
- items_out: float32 [131072, 256], P('strat')
Inputs may be any that keep to these rules, and one draw needn't show every extreme that they name: `tile_coords`: each list names distinct tiles; user tiles lie below 8 and item tiles below 32; entries at and after the count are ignored. `tile_counts`: in every sub-epoch some device has exactly 16 live tiles.
All inputs are finite; a program needn't handle non-finite values.
Results may differ from a plain program's by a relative error of at most 0.0018.
Values sent between devices are 32-bit elements; how exact they have to be, the bound alone decides.
A program may use at most 64 MiB of HBM per device.

v0:
```python
import jax
import jax.numpy as jnp
from jax import lax
from jax.sharding import PartitionSpec as P


def from_behind(block, axis, distance):
    devices = range(lax.axis_size(axis))
    route = [((i - distance) % len(devices), i) for i in devices]
    return lax.ppermute(block, axis, route)


def tile_terms(user_b, slab_b, coords, count, values):
    high = lax.Precision.HIGHEST
    side = values.shape[-1]
    width = user_b.shape[1]
    user_tiles = user_b.shape[0] // side
    item_tiles = slab_b.shape[0] // side
    urows = jnp.take(user_b.reshape(user_tiles, side, width), coords[0], axis=0)
    irows = jnp.take(slab_b.reshape(item_tiles, side, width), coords[1], axis=0)
    predicted = jnp.einsum("nrk,nck->nrc", urows, irows, preferred_element_type=jnp.float32)
    resid = (values.astype(jnp.float32) - predicted).astype(jnp.bfloat16)
    user_part = jnp.einsum("nrc,nck->nrk", resid, irows, preferred_element_type=jnp.float32)
    item_part = jnp.einsum("nrc,nrk->nck", resid, urows, preferred_element_type=jnp.float32)
    live = jnp.arange(coords.shape[1]) < count
    one_user = ((coords[0][:, None] == jnp.arange(user_tiles)[None, :]) & live[:, None]).astype(
        jnp.float32
    )
    one_item = ((coords[1][:, None] == jnp.arange(item_tiles)[None, :]) & live[:, None]).astype(
        jnp.float32
    )
    user_grad = jnp.einsum("nt,nrk->trk", one_user, user_part, precision=high).reshape(-1, width)
    item_grad = jnp.einsum("nt,nrk->trk", one_item, item_part, precision=high).reshape(-1, width)
    return (user_grad, item_grad)


def per_device(user_factors, item_factors, tile_coords, tile_counts, tile_values):
    users = user_factors
    slab = item_factors
    coords = tile_coords[0, 0]
    counts = tile_counts[0, 0]
    values = tile_values[0, 0]
    rounds = coords.shape[0]
    for sub in range(rounds):
        user_grad, item_grad = tile_terms(
            users.astype(jnp.bfloat16),
            slab.astype(jnp.bfloat16),
            coords[sub],
            counts[sub],
            values[sub],
        )
        users = users - 0.003 * (0.05 * users - user_grad)
        total = lax.psum(item_grad, "grp")
        slab = slab - 0.003 * (0.05 * slab - total)
        if sub + 1 < rounds:
            slab = from_behind(slab, "strat", -1)
    return (users, slab)


def solution(mesh):
    placed = (
        P(("strat", "grp"), None),
        P("strat", None),
        P("strat", "grp", None, None, None),
        P("strat", "grp", None),
        P("strat", "grp", None, None, None, None),
    )
    return jax.shard_map(
        per_device,
        mesh=mesh,
        in_specs=placed,
        out_specs=(P(("strat", "grp"), None), P("strat", None)),
        check_vma=False,
    )
```

profile of v0, /device:TPU:1, one launch (start us, length us, event | category | flops | bytes accessed | tf_op | source)
XLA Modules:
  0.0 752.5 jit_solution(12786251001411020271)
XLA Ops:
  12.1 2.4 convert_element_type.54
  16.7 2.0 fusion.12
  19.2 2.9 fusion.8
  22.1 4.4 copy.8
  26.6 190.7 %all-reduce.4.cloned.1.call-done = f32[4096,256]{1,0:T(8,128)} async-done(((f32[4096,256]{1,0:T(8,128)}), f32[4096,256]{1,0:T(8,128)}) %all-reduce.4.cloned.1.call-update) | async-done | bytes 4194320 | tf_op jit(solution)/shard_map/psum | solution.py:53
  217.3 6.2 multiply_subtract_fusion.2
  229.5 43.7 %collective-permute-done = f32[4096,256]{1,0:T(8,128)} collective-permute-done((f32[4096,256]{1,0:T(8,128)}, f32[4096,256]{1,0:T(8,128)}, u32[]{:S(2)}, u32[]{:S(2)}) %collective-permute-start) | collective-permute-done | bytes 4194336 | tf_op jit(solution)/shard_map/ppermute | solution.py:10
  273.2 3.7 convert_element_type.59
  276.9 2.2 gather_fusion.3
  281.9 2.9 fusion.4
  284.9 4.4 copy.10
  289.4 188.5 %all-reduce.6.cloned.1.call-done = f32[4096,256]{1,0:T(8,128)} async-done(((f32[4096,256]{1,0:T(8,128)}), f32[4096,256]{1,0:T(8,128)}) %all-reduce.6.cloned.1.call-update) | async-done | bytes 4194320 | tf_op jit(solution)/shard_map/psum | solution.py:53
  477.9 6.2 multiply_subtract_fusion.1
  486.1 2.0 fusion.6
  489.5 2.6 gather_fusion.4
  492.1 41.7 %collective-permute-done.1 = f32[4096,256]{1,0:T(8,128)} collective-permute-done((f32[4096,256]{1,0:T(8,128)}, f32[4096,256]{1,0:T(8,128)}, u32[]{:S(2)}, u32[]{:S(2)}) %collective-permute-start.1) | collective-permute-done | bytes 4194336 | tf_op jit(solution)/shard_map/ppermute | solution.py:10
  533.8 3.7 convert_element_type.64
  537.5 3.3 gather_fusion.5
  540.8 2.3 fusion.14
  543.9 2.9 fusion
  546.8 4.4 copy.12
  553.2 2.0 fusion.2
  556.9 182.9 %all-reduce.8.cloned.1.call-done = f32[4096,256]{1,0:T(8,128)} async-done(((f32[4096,256]{1,0:T(8,128)}), f32[4096,256]{1,0:T(8,128)}) %all-reduce.8.cloned.1.call-update) | async-done | bytes 4194320 | tf_op jit(solution)/shard_map/psum | solution.py:53
  739.8 6.2 multiply_subtract_fusion
  (49 shorter events, 24.3 us)
Async XLA Ops:
  7.2 210.1 %all-reduce.4.cloned.1.call-start = ((), (), s32[]{:S(2)}) async-start(), calls=%async_computation | async-start | bytes 8388608 | tf_op jit(solution)/shard_map/psum | solution.py:53
  16.7 2.0 copy-start.3
  26.6 451.3 %all-reduce.6.cloned.1.call-start = ((), (), s32[]{:S(2)}) async-start(), calls=%async_computation.1 | async-start | bytes 8388608 | tf_op jit(solution)/shard_map/psum | solution.py:53
  223.5 49.8 %collective-permute-start = (f32[4096,256]{1,0:T(8,128)}, f32[4096,256]{1,0:T(8,128)}, u32[]{:S(2)}, u32[]{:S(2)}) collective-permute-start(f32[4096,256]{1,0:T(8,128)} %multiply_subtract_fusion.2), channel_id=1, source_target_pairs={{8,0},{16,8},{24,16},{32,24},{40,32},{48,40},{56,48},{64,56},{72,6... | collective-permute-start | bytes 12582920 | tf_op jit(solution)/shard_map/ppermute | solution.py:10
  224.8 2.4 copy-start
  279.1 2.0 copy-start.1
  281.1 0.8 copy-start.4
  289.3 450.5 %all-reduce.8.cloned.1.call-start = ((), (), s32[]{:S(2)}) async-start(), calls=%async_computation.2 | async-start | bytes 8388608 | tf_op jit(solution)/shard_map/psum | solution.py:53
  477.9 7.7 %copy-start.5 = (bf16[16,128,128]{2,1,0:T(8,128)(2,1)S(1)}, bf16[16,128,128]{2,1,0:T(8,128)(2,1)}, u32[]{:S(2)}) copy-start(bf16[16,128,128]{2,1,0:T(8,128)(2,1)} %copy-done.4) | copy-start | bytes 1572868
  484.1 49.8 %collective-permute-start.1 = (f32[4096,256]{1,0:T(8,128)}, f32[4096,256]{1,0:T(8,128)}, u32[]{:S(2)}, u32[]{:S(2)}) collective-permute-start(f32[4096,256]{1,0:T(8,128)} %multiply_subtract_fusion.1), channel_id=1, source_target_pairs={{8,0},{16,8},{24,16},{32,24},{40,32},{48,40},{56,48},{64,56},{72,6... | collective-permute-start | bytes 12582920 | tf_op jit(solution)/shard_map/ppermute | solution.py:10
  540.8 2.3 copy-start.2
  543.1 0.8 copy-start.6
Sparse Core Ops, SparseCore 0:
  26.7 190.5 all-reduce.3
  289.4 188.3 all-reduce.5
  551.4 188.3 all-reduce.7
where the time goes:
time: 753 us
  waiting for transfers between devices  648 us (86%)
  other arithmetic  34.9 us (5%)
  local copies, waits for them, and re-layouts  28.9 us (4%)
  matrix products  25.3 us (3%)
  between operations  14 us (2%)
    psum x3, waiting for transfers between devices, per_device(): total = lax.psum(item_grad, 'grp')  562 us
    ppermute x2, waiting for transfers between devices, from_behind(): return lax.ppermute(block, axis, route)  85.4 us
    sub x3, other arithmetic, per_device(): slab = slab - 0.003 * (0.05 * slab - total)  18.5 us
  transfers between devices with their start and end apart: 5, of which 5 were waited for; matrix products, arithmetic and copies ran while one was open for 2% of the time, Pallas kernels for 0%

commit v1 on v0

--- a/solution.py
+++ b/solution.py
@@ -50,7 +50,8 @@
             values[sub],
         )
         users = users - 0.003 * (0.05 * users - user_grad)
-        total = lax.psum(item_grad, "grp")
+        pieces = lax.all_gather(item_grad, "grp", axis=0, tiled=False)
+        total = pieces.sum(axis=0)
         slab = slab - 0.003 * (0.05 * slab - total)
         if sub + 1 < rounds:
             slab = from_behind(slab, "strat", -1)

time: 753 us -> 2170 us (2.88)
  waiting for transfers between devices: 648 us -> 2010 us
  other arithmetic: 34.9 us -> 77.9 us
    all_gather x0 -> x3, waiting for transfers between devices: none -> 1930 us  [per_device(): pieces = lax.all_gather(item_grad, 'grp', axis=0, tiled=False)]
    psum x3 -> x0, waiting for transfers between devices: 562 us -> none  [per_device(): total = lax.psum(item_grad, 'grp')]
    reduce_sum x0 -> x3, other arithmetic: none -> 43 us  [per_device(): total = pieces.sum(axis=0)]
  transfers between devices with their start and end apart: 5 -> 5, of which waited for: 5 -> 5; matrix products, arithmetic and copies ran while one was open for 2% -> 1% of each run, Pallas kernels for 0% -> 0%
where the time goes in v1:
time: 2170 us; the launch traced here: 2160 us
  waiting for transfers between devices  2010 us (93%)
  other arithmetic  77.9 us (4%)
  local copies, waits for them, and re-layouts  28.9 us (1%)
  matrix products  25.5 us (1%)
    all_gather x3, waiting for transfers between devices, per_device(): pieces = lax.all_gather(item_grad, 'grp', axis=0, tiled=False)  1930 us
    ppermute x2, waiting for transfers between devices, from_behind(): return lax.ppermute(block, axis, route)  85.4 us
  transfers between devices with their start and end apart: 5, of which 5 were waited for; matrix products, arithmetic and copies ran while one was open for 1% of the time, Pallas kernels for 0%

profile of v1, /device:TPU:1, one launch (start us, length us, event | category | flops | bytes accessed | tf_op | source)
XLA Modules:
  0.0 2163.9 jit_solution(13051618496336947924)
XLA Ops:
  12.1 2.4 convert_element_type.54
  19.2 2.9 fusion.8
  22.1 4.4 copy.17
  26.7 646.5 %all-gather.4.cloned.1.call-done = f32[8,4096,256]{2,1,0:T(8,128)} async-done(((f32[1,4096,256]{2,1,0:T(8,128)}), f32[8,4096,256]{2,1,0:T(8,128)}) %all-gather.4.cloned.1.call-update) | async-done | bytes 33554448 | tf_op jit(solution)/shard_map/all_gather | solution.py:53
  673.1 14.3 reduce_sum.27
  687.5 6.2 multiply_subtract_fusion.2
  700.2 43.6 %collective-permute-done = f32[4096,256]{1,0:T(8,128)} collective-permute-done((f32[4096,256]{1,0:T(8,128)}, f32[4096,256]{1,0:T(8,128)}, u32[]{:S(2)}, u32[]{:S(2)}) %collective-permute-start) | collective-permute-done | bytes 4194336 | tf_op jit(solution)/shard_map/ppermute | solution.py:10
  743.8 3.7 convert_element_type.59
  747.5 2.2 gather_fusion.3
  752.5 2.9 fusion.4
  755.5 4.4 copy.22
  760.0 644.4 %all-gather.6.cloned.1.call-done = f32[8,4096,256]{2,1,0:T(8,128)} async-done(((f32[1,4096,256]{2,1,0:T(8,128)}), f32[8,4096,256]{2,1,0:T(8,128)}) %all-gather.6.cloned.1.call-update) | async-done | bytes 33554448 | tf_op jit(solution)/shard_map/all_gather | solution.py:53
  1404.4 14.3 reduce_sum.28
  1418.7 6.2 multiply_subtract_fusion.1
  1430.4 2.6 gather_fusion.4
  1433.0 41.8 %collective-permute-done.1 = f32[4096,256]{1,0:T(8,128)} collective-permute-done((f32[4096,256]{1,0:T(8,128)}, f32[4096,256]{1,0:T(8,128)}, u32[]{:S(2)}, u32[]{:S(2)}) %collective-permute-start.1) | collective-permute-done | bytes 4194336 | tf_op jit(solution)/shard_map/ppermute | solution.py:10
  1474.8 3.7 convert_element_type.64
  1478.5 3.2 gather_fusion.5
  1481.7 2.3 fusion.14
  1484.8 2.9 fusion
  1487.7 4.4 copy.27
  1498.0 638.6 %all-gather.8.cloned.1.call-done = f32[8,4096,256]{2,1,0:T(8,128)} async-done(((f32[1,4096,256]{2,1,0:T(8,128)}), f32[8,4096,256]{2,1,0:T(8,128)}) %all-gather.8.cloned.1.call-update) | async-done | bytes 33554448 | tf_op jit(solution)/shard_map/all_gather | solution.py:53
  2136.6 14.3 reduce_sum.29
  2151.0 6.2 multiply_subtract_fusion
  (52 shorter events, 31.0 us)
Async XLA Ops:
  7.2 666.0 %all-gather.4.cloned.1.call-start = ((), (), s32[]{:S(2)}) async-start(), calls=%async_computation | async-start | bytes 37748736 | tf_op jit(solution)/shard_map/all_gather | solution.py:53
  16.7 2.0 copy-start.3
  26.6 1377.8 %all-gather.6.cloned.1.call-start = ((), (), s32[]{:S(2)}) async-start(), calls=%async_computation.1 | async-start | bytes 37748736 | tf_op jit(solution)/shard_map/all_gather | solution.py:53
  693.6 50.2 %collective-permute-start = (f32[4096,256]{1,0:T(8,128)}, f32[4096,256]{1,0:T(8,128)}, u32[]{:S(2)}, u32[]{:S(2)}) collective-permute-start(f32[4096,256]{1,0:T(8,128)} %multiply_subtract_fusion.2), channel_id=1, source_target_pairs={{8,0},{16,8},{24,16},{32,24},{40,32},{48,40},{56,48},{64,56},{72,6... | collective-permute-start | bytes 12582920 | tf_op jit(solution)/shard_map/ppermute | solution.py:10
  695.4 2.4 copy-start
  749.7 2.0 copy-start.1
  751.7 0.8 copy-start.4
  759.9 1376.7 %all-gather.8.cloned.1.call-start = ((), (), s32[]{:S(2)}) async-start(), calls=%async_computation.2 | async-start | bytes 37748736 | tf_op jit(solution)/shard_map/all_gather | solution.py:53
  1418.7 7.8 copy-start.5
  1424.9 49.9 %collective-permute-start.1 = (f32[4096,256]{1,0:T(8,128)}, f32[4096,256]{1,0:T(8,128)}, u32[]{:S(2)}, u32[]{:S(2)}) collective-permute-start(f32[4096,256]{1,0:T(8,128)} %multiply_subtract_fusion.1), channel_id=1, source_target_pairs={{8,0},{16,8},{24,16},{32,24},{40,32},{48,40},{56,48},{64,56},{72,6... | collective-permute-start | bytes 12582920 | tf_op jit(solution)/shard_map/ppermute | solution.py:10
  1481.7 2.3 copy-start.2
  1484.0 0.8 copy-start.6
Sparse Core Ops, SparseCore 0:
  26.7 646.3 all-gather.3
  760.0 644.2 all-gather.5
  1492.3 644.2 all-gather.7
